TPU v7x, 32 devices: a whole 2x2x4 slice. The times are simulated.
32 devices in a mesh: box: 2 (over y), gx: 8 (over z, x), gy: 2 (over core).
Axes of the slice: x: 2, y: 2, z: 4, core: 2. Of those that a mesh axis runs over, the one named last changes fastest.
Arguments:
- positions: float32 [16, 4, 3, 256], P(('box', 'gx'), 'gy'), parts along dimension 0, may hold values from 0 to 18, as said below
- polarizability: float32 [16, 4, 256], P(('box', 'gx'), 'gy'), parts along dimension 0, may hold values from 0.3 to 1.5
- tile_counts: int32 [16, 4, 2], P(('box', 'gx'), 'gy'), parts along dimension 0, may hold values from 80 to 128, as said below
- molecules: int32 [16, 4, 256], P(('box', 'gx'), 'gy'), parts along dimension 0, may hold values from 0 to 170, as said below
- perm_field: float32 [16, 4, 3, 256], P(('box', 'gx'), 'gy'), parts along dimension 0, may hold values from -6 to 6
- dipoles: float32 [16, 4, 3, 256], P(('box', 'gx'), 'gy'), parts along dimension 0, may hold values from -4 to 4
- past_out: float32 [16, 4, 7, 3, 256], P(('box', 'gx'), 'gy'), parts along dimension 0, may hold values from -4 to 4
- past_res: float32 [16, 4, 7, 3, 256], P(('box', 'gx'), 'gy'), parts along dimension 0, may hold values from -15 to 15
Outputs:
- dipoles_next: float32 [16, 4, 3, 256], P(('box', 'gx'), 'gy'), parts along dimension 0
- diis_weights: float32 [16], P('box'), parts along dimension 0
There are 2 independent parts, one for each index of `box`. A program takes and returns all parts, laid end to end along the dimension named above; each array names one. Nothing has to cross between parts.
Inputs may be any that keep to these rules, and one draw needn't show every extreme that they name: x and y in [0, 9); z of an atom in z-tile t lies in [9 t, 9 t + 9); padded slots carry positions too. `tile_counts`: some z-tile is full. `molecules`: a group holds at most three atoms, all of one z-tile of one cell.
All inputs are finite; a program needn't handle non-finite values.
Results may differ from a plain program's by a relative error of at most 0.0003.
Values sent between devices are 32-bit elements; how exact they have to be, the bound alone decides.
A program may use at most 64 MiB of HBM per device.

v0:
```python
import jax
import jax.numpy as jnp
from jax import lax
from jax.sharding import PartitionSpec as P

ITERS = 2
CELL_SIDE = 9.0
CUTOFF_SQ = 81.0
SOFTENING = 0.25
THOLE_DAMP = 0.39
FAR_LIFT = 1000.0
NEIGHBOUR_X = (1.0, 0.0, 1.0, 1.0)
NEIGHBOUR_Y = (0.0, 1.0, 1.0, -1.0)


def from_behind(block, axis, distance):
    devices = range(lax.axis_size(axis))
    route = [((i - distance) % len(devices), i) for i in devices]
    return lax.ppermute(block, axis, route)


def pair_terms(
    target_coords,
    target_polar,
    target_groups,
    target_occupied,
    source_coords,
    source_polar,
    source_groups,
    source_occupied,
):
    displace = source_coords[:, None, :] - target_coords[:, :, None]
    square_dist = jnp.sum(displace * displace, axis=0) + SOFTENING
    distance = jnp.sqrt(square_dist)
    cube_dist = square_dist * distance
    damped = THOLE_DAMP * cube_dist / jnp.sqrt(target_polar[:, None] * source_polar[None, :])
    damping = jnp.exp(-damped)
    tapering = jnp.square(jnp.maximum(1.0 - square_dist / CUTOFF_SQ, 0.0))
    keeper = (target_groups[:, None] != source_groups[None, :]).astype(jnp.float32)
    weight = tapering * keeper * target_occupied[:, None] * source_occupied[None, :]
    isotropic = weight * -jnp.expm1(-damped) / cube_dist
    tensorial = 3.0 * weight * (1.0 - (1.0 + damped) * damping) / (cube_dist * square_dist)
    return (displace, isotropic, tensorial)


def field_targets(displace, isotropic, tensorial, source_dipole):
    projected = jnp.sum(displace * source_dipole[:, None, :], axis=0)
    return jnp.sum(displace * (tensorial * projected)[None], axis=2) - jnp.sum(
        isotropic[None] * source_dipole[:, None, :], axis=2
    )


def field_sources(displace, isotropic, tensorial, target_dipole):
    projected = jnp.sum(displace * target_dipole[:, :, None], axis=0)
    return jnp.sum(displace * (tensorial * projected)[None], axis=1) - jnp.sum(
        isotropic[None] * target_dipole[:, :, None], axis=1
    )


def tiled(values, filler, tile_count):
    shaped = values.reshape(values.shape[:-1] + (tile_count, values.shape[-1] // tile_count))
    widths = [(0, 0)] * (shaped.ndim - 2) + [(1, 1), (0, 0)]
    return jnp.pad(shaped, widths, constant_values=filler)


def padded_coords(coords, tile_count):
    marker = tiled(jnp.zeros_like(coords), 1.0, tile_count)
    lifted = jnp.array([0.0, 0.0, FAR_LIFT], jnp.float32).reshape(3, 1, 1)
    return tiled(coords, 0.0, tile_count) + marker * lifted


def band_sources(padded, tile_at):
    coords, polarity, groups, occupied, dipole = padded

    def flat_vector(member):
        window_part = lax.dynamic_slice_in_dim(member, tile_at, 3, 2)
        return jnp.transpose(window_part, (1, 0, 2, 3)).reshape(3, -1)

    def flat_scalar(member):
        return lax.dynamic_slice_in_dim(member, tile_at, 3, 1).reshape(-1)

    return (
        flat_vector(coords),
        flat_scalar(polarity),
        flat_scalar(groups),
        flat_scalar(occupied),
        flat_vector(dipole),
    )


def target_tile(own_cell, first_slot, tile_width):
    coords, polarity, groups, occupied = own_cell
    return (
        lax.dynamic_slice_in_dim(coords, first_slot, tile_width, 1),
        lax.dynamic_slice_in_dim(polarity, first_slot, tile_width, 0),
        lax.dynamic_slice_in_dim(groups, first_slot, tile_width, 0),
        lax.dynamic_slice_in_dim(occupied, first_slot, tile_width, 0),
    )


def four_static(packed):
    east_cells = from_behind(packed, "gx", -1)
    next_own, next_east = from_behind((packed[0], east_cells[0]), "gy", -1)
    prior_east = from_behind(east_cells[-1], "gy", 1)
    north_cells = jnp.concatenate([packed[1:], next_own[None]], axis=0)
    north_east = jnp.concatenate([east_cells[1:], next_east[None]], axis=0)
    south_east = jnp.concatenate([prior_east[None], east_cells[:-1]], axis=0)
    return jnp.stack([east_cells, north_cells, north_east, south_east], axis=1)


def four_dipole(dipole):
    east_cells = from_behind(dipole, "gx", -1)
    next_own, next_east = from_behind((dipole[0], east_cells[0]), "gy", -1)
    prior_east = from_behind(east_cells[-1], "gy", 1)
    north_cells = jnp.concatenate([dipole[1:], next_own[None]], axis=0)
    north_east = jnp.concatenate([east_cells[1:], next_east[None]], axis=0)
    south_east = jnp.concatenate([prior_east[None], east_cells[:-1]], axis=0)
    return jnp.stack([east_cells, north_cells, north_east, south_east], axis=1)


def half_statics(coords, polarity, groups, occupied, tile_count):
    cell_count = coords.shape[0]
    packed = jnp.concatenate([coords, polarity[:, None], occupied[:, None]], axis=1)
    nearby = four_static(packed)
    lift_x = jnp.array(NEIGHBOUR_X, jnp.float32) * CELL_SIDE
    lift_y = jnp.array(NEIGHBOUR_Y, jnp.float32) * CELL_SIDE
    lifted = jnp.stack([lift_x, lift_y, jnp.zeros_like(lift_x)], axis=1)
    nearby_coords = nearby[:, :, 0:3] + lifted[None, :, :, None]
    nearby_groups = jnp.full((cell_count, 4, coords.shape[-1]), -1, jnp.int32)
    own_padded = (
        padded_coords(coords[:, None], tile_count),
        tiled(polarity[:, None], 1.0, tile_count),
        tiled(groups[:, None], -1, tile_count),
        tiled(occupied[:, None], 0.0, tile_count),
    )
    nearby_padded = (
        padded_coords(nearby_coords, tile_count),
        tiled(nearby[:, :, 3], 1.0, tile_count),
        tiled(nearby_groups, -1, tile_count),
        tiled(nearby[:, :, 4], 0.0, tile_count),
    )
    return (own_padded, nearby_padded)


def half_cell(own_cell, own_band, nearby_band, dipole, tile_count):
    tile_width = dipole.shape[-1] // tile_count

    def one_tile(tile_at, carry):
        own_field, back_field = carry
        first_slot = tile_at * tile_width
        target = target_tile(own_cell, first_slot, tile_width)
        target_dipole = lax.dynamic_slice_in_dim(dipole, first_slot, tile_width, 1)
        source = band_sources(own_band, tile_at)
        displace, isotropic, tensorial = pair_terms(
            target[0], target[1], target[2], target[3], source[0], source[1], source[2], source[3]
        )
        inside = field_targets(displace, isotropic, tensorial, source[4])
        source = band_sources(nearby_band, tile_at)
        displace, isotropic, tensorial = pair_terms(
            target[0], target[1], target[2], target[3], source[0], source[1], source[2], source[3]
        )
        outside = field_targets(displace, isotropic, tensorial, source[4])
        returned = field_sources(displace, isotropic, tensorial, target_dipole)
        returned = jnp.transpose(returned.reshape(3, 4, 3, tile_width), (1, 0, 2, 3))
        own_field = lax.dynamic_update_slice_in_dim(own_field, inside + outside, first_slot, 1)
        window = lax.dynamic_slice_in_dim(back_field, tile_at, 3, 2) + returned
        back_field = lax.dynamic_update_slice_in_dim(back_field, window, tile_at, 2)
        return (own_field, back_field)

    initial = (
        jnp.zeros(dipole.shape, jnp.float32),
        jnp.zeros((4, 3, tile_count + 2, tile_width), jnp.float32),
    )
    own_field, back_field = lax.fori_loop(0, tile_count, one_tile, initial)
    return (own_field, back_field[:, :, 1:-1].reshape(4, 3, -1))


def half_field(own_cells, statics, dipole, tile_count):
    own_padded, nearby_padded = statics
    own_band = own_padded + (tiled(dipole[:, None], 0.0, tile_count),)
    nearby_band = nearby_padded + (tiled(four_dipole(dipole), 0.0, tile_count),)

    def per_cell(members):
        return half_cell(members[0], members[1], members[2], members[3], tile_count)

    own_field, back_field = lax.map(per_cell, (own_cells, own_band, nearby_band, dipole))
    north_part = back_field[:, 1]
    north_east = back_field[:, 2]
    south_east = back_field[:, 3]
    from_below, below_east = from_behind((north_part[-1], north_east[-1]), "gy", 1)
    from_above = from_behind(south_east[0], "gy", -1)
    from_south = jnp.concatenate([from_below[None], north_part[:-1]], axis=0)
    from_south_west = jnp.concatenate([below_east[None], north_east[:-1]], axis=0)
    from_north = jnp.concatenate([south_east[1:], from_above[None]], axis=0)
    eastward = back_field[:, 0] + from_south_west + from_north
    from_west = from_behind(eastward, "gx", 1)
    return own_field + from_south + from_west


def diis_weights(gram_matrix):
    lower = jnp.linalg.cholesky(gram_matrix)
    history = gram_matrix.shape[0]
    forward = []
    for row_at in range(history):
        running = jnp.ones((), gram_matrix.dtype)
        for col_at in range(row_at):
            running = running - lower[row_at, col_at] * forward[col_at]
        forward.append(running / lower[row_at, row_at])
    backward = [None] * history
    for row_at in reversed(range(history)):
        running = forward[row_at]
        for col_at in range(row_at + 1, history):
            running = running - lower[col_at, row_at] * backward[col_at]
        backward[row_at] = running / lower[row_at, row_at]
    solved = jnp.stack(backward)
    return solved / jnp.sum(solved)


def body(
    positions, polarizability, tile_counts, molecules, perm_field, dipoles, past_out, past_res
):
    counts = tile_counts[0]
    cell_count = counts.shape[0]
    tile_count = counts.shape[1]
    coords = positions[0]
    atom_slots = coords.shape[-1]
    tile_width = atom_slots // tile_count
    slot_index = lax.broadcasted_iota(jnp.int32, (cell_count, tile_count, tile_width), 2)
    occupied = (slot_index < counts[:, :, None]).astype(jnp.float32).reshape(cell_count, atom_slots)
    polarity = polarizability[0]
    groups = molecules[0]
    own_cells = (coords, polarity, groups, occupied)
    occupied_vec = occupied[:, None, :]
    scaled = occupied_vec * polarity[:, None, :]
    stored_out = jnp.moveaxis(past_out[0], 1, 0) * occupied_vec
    stored_res = jnp.moveaxis(past_res[0], 1, 0) * occupied_vec
    current = dipoles[0] * occupied_vec
    permanent = perm_field[0]
    statics = half_statics(coords, polarity, groups, occupied, tile_count)
    weights = jnp.zeros((stored_out.shape[0] + 1,), jnp.float32)
    for step_at in range(ITERS):
        induced = half_field(own_cells, statics, current, tile_count)
        jacobi = scaled * (permanent + induced)
        residual = jacobi - current
        outputs_all = jnp.concatenate([stored_out, jacobi[None]], 0)
        residual_all = jnp.concatenate([stored_res, residual[None]], 0)
        flattened = residual_all.reshape(residual_all.shape[0], -1)
        local_gram = jnp.dot(
            flattened,
            flattened.T,
            precision=lax.Precision.HIGHEST,
            preferred_element_type=jnp.float32,
        )
        gram_matrix = lax.psum(local_gram, ("gx", "gy"))
        weights = diis_weights(gram_matrix)
        current = jnp.sum(weights[:, None, None, None] * outputs_all, axis=0)
        stored_out = outputs_all[1:]
        stored_res = residual_all[1:]
    return (current[None], weights)


def solution(mesh):
    placed = (
        P(("box", "gx"), "gy", None, None),
        P(("box", "gx"), "gy", None),
        P(("box", "gx"), "gy", None),
        P(("box", "gx"), "gy", None),
        P(("box", "gx"), "gy", None, None),
        P(("box", "gx"), "gy", None, None),
        P(("box", "gx"), "gy", None, None, None),
        P(("box", "gx"), "gy", None, None, None),
    )
    return jax.shard_map(
        body,
        mesh=mesh,
        in_specs=placed,
        out_specs=(P(("box", "gx"), "gy", None, None), P("box")),
        check_vma=False,
    )
```

profile of v0, /device:TPU:0, one launch (start us, length us, event | category | flops | bytes accessed | tf_op | source)
XLA Modules:
  0.0 246.8 jit_solution(973416661079791287)
XLA Ops:
  2.1 6.0 %collective-permute-start.4 = (f32[2,3,256]{2,1,0:T(4,128)S(1)}, f32[2,3,256]{2,1,0:T(4,128)S(1)}, u32[]{:S(2)}, u32[]{:S(2)}) collective-permute-start(f32[2,3,256]{2,1,0:T(4,128)S(1)} %bitcast_multiply_fusion.2), channel_id=1, source_target_pairs={{2,0},{4,2},{6,4},{8,6},{10,8},{12,10},{14,12},{0,14},{3,1},{5,3},... | collective-permute-start | bytes 18440 | tf_op jit(solution)/shard_map/ppermute | solution.py:19
  20.0 23.1 %while.55 = (s32[]{:T(128)}, f32[2,3,256]{2,1,0:T(4,128)S(1)}, f32[2,4,3,256]{3,1,2,0:T(4,128)S(1)}, f32[2,3,256]{2,1,0:T(4,128)S(1)}, f32[2,256]{1,0:T(2,128)S(...) while((s32[]{:T(128)}, f32[2,3,256]{2,1,0:T(4,128)S(1)}, ...), condition=%wide.region_14.15_spmd, body=%wide.region_0.14_spmd.sunk | while | flops 19906180 | bytes 14344956 | solution.py:186
  20.2 11.3 %while.58 = (s32[]{:T(128)}, f32[3,256]{1,0:T(4,128)S(1)}, f32[4,3,4,128]{3,2,0,1:T(4,128)S(1)}, f32[1,3,4,128]{3,2,1,0:T(4,128)S(1)}, f32[3,256]{1,0:T(4,128)S(...) while((s32[]{:T(128)}, f32[3,256]{1,0:T(4,128)S(1)}, ...), condition=%wide.region_13.13_spmd, body=%wide.region_1.12_spmd.sunk | while | flops 19906180 | bytes 14031151 | solution.py:174
  21.9 1.0 fusion.153
  22.8 1.0 fusion.154
  23.8 1.0 fusion.155
  27.5 1.0 fusion.153
  28.5 1.0 fusion.154
  29.5 1.0 fusion.155
  31.7 11.3 %while.58 = (s32[]{:T(128)}, f32[3,256]{1,0:T(4,128)S(1)}, f32[4,3,4,128]{3,2,0,1:T(4,128)S(1)}, f32[1,3,4,128]{3,2,1,0:T(4,128)S(1)}, f32[3,256]{1,0:T(4,128)S(...) while((s32[]{:T(128)}, f32[3,256]{1,0:T(4,128)S(1)}, ...), condition=%wide.region_13.13_spmd, body=%wide.region_1.12_spmd.sunk | while | flops 19906180 | bytes 14031151 | solution.py:174
  33.4 1.0 fusion.153
  34.4 1.0 fusion.154
  35.4 1.0 fusion.155
  39.0 1.0 fusion.153
  40.0 1.0 fusion.154
  44.7 1.5 collective-permute-start.11
  46.2 4.8 %collective-permute-done.11 = f32[2,3,256]{2,1,0:T(4,128)S(1)} collective-permute-done((f32[2,3,256]{2,1,0:T(4,128)S(1)}, f32[2,3,256]{2,1,0:T(4,128)S(1)}, u32[]{:S(2)}, u32[]{:S(2)}) %collective-permute-start.11) | collective-permute-done | bytes 6176 | tf_op jit(solution)/shard_map/ppermute | solution.py:19
  51.3 29.5 %psum.14 = f32[8,8]{0,1:T(8,128)S(1)} all-reduce(f32[8,8]{0,1:T(8,128)S(1)} %convolution_bitcast_fusion.1), channel_id=1, replica_groups=mesh['box'=2,'gx'=8,'gy'=2] {'gx','gy'}, use_global_device_ids=true, to_apply=%region_15.16 | all-reduce | flops 64 | bytes 512 | tf_op jit(solution)/shard_map/psum | solution.py:254
  130.7 3.5 %collective-permute-done.12 = f32[2,3,256]{2,1,0:T(4,128)S(1)} collective-permute-done((f32[2,3,256]{2,1,0:T(4,128)S(1)}, f32[2,3,256]{2,1,0:T(4,128)S(1)}, u32[]{:S(2)}, u32[]{:S(2)}) %collective-permute-start.12) | collective-permute-done | bytes 6176 | tf_op jit(solution)/shard_map/ppermute | solution.py:19
  135.7 23.1 %while.57 = (s32[]{:T(128)}, f32[2,3,256]{2,1,0:T(4,128)S(1)}, f32[2,4,3,256]{3,1,2,0:T(4,128)S(1)}, f32[2,3,256]{2,1,0:T(4,128)S(1)}, f32[2,256]{1,0:T(2,128)S(...) while((s32[]{:T(128)}, f32[2,3,256]{2,1,0:T(4,128)S(1)}, ...), condition=%wide.region_33.35_spmd, body=%wide.region_19.34_spmd.sunk | while | flops 19906180 | bytes 14344960 | solution.py:186
  135.9 11.3 %while.59 = (s32[]{:T(128)}, f32[3,256]{1,0:T(4,128)S(1)}, f32[4,3,4,128]{3,2,0,1:T(4,128)S(1)}, f32[1,3,4,128]{3,2,1,0:T(4,128)S(1)}, f32[3,256]{1,0:T(4,128)S(...) while((s32[]{:T(128)}, f32[3,256]{1,0:T(4,128)S(1)}, ...), condition=%wide.region_32.33_spmd, body=%wide.region_20.32_spmd.sunk | while | flops 19906180 | bytes 14031151 | solution.py:174
  137.6 1.0 fusion.143
  138.6 1.0 fusion.144
  143.2 1.0 fusion.143
  144.2 1.0 fusion.144
  147.5 11.3 %while.59 = (s32[]{:T(128)}, f32[3,256]{1,0:T(4,128)S(1)}, f32[4,3,4,128]{3,2,0,1:T(4,128)S(1)}, f32[1,3,4,128]{3,2,1,0:T(4,128)S(1)}, f32[3,256]{1,0:T(4,128)S(...) while((s32[]{:T(128)}, f32[3,256]{1,0:T(4,128)S(1)}, ...), condition=%wide.region_32.33_spmd, body=%wide.region_20.32_spmd.sunk | while | flops 19906180 | bytes 14031151 | solution.py:174
  149.2 1.0 fusion.143
  150.2 1.0 fusion.144
  154.8 1.0 fusion.143
  155.8 1.0 fusion.144
  160.7 6.1 %collective-permute-done.19 = f32[2,3,256]{2,1,0:T(4,128)S(1)} collective-permute-done((f32[2,3,256]{2,1,0:T(4,128)S(1)}, f32[2,3,256]{2,1,0:T(4,128)S(1)}, u32[]{:S(2)}, u32[]{:S(2)}) %collective-permute-start.19) | collective-permute-done | bytes 6176 | tf_op jit(solution)/shard_map/ppermute | solution.py:19
  167.1 29.5 %psum.15 = f32[8,8]{0,1:T(8,128)S(1)} all-reduce(f32[8,8]{0,1:T(8,128)S(1)} %convolution_bitcast_fusion), channel_id=1, replica_groups=mesh['box'=2,'gx'=8,'gy'=2] {'gx','gy'}, use_global_device_ids=true, to_apply=%region_34.36 | all-reduce | flops 64 | bytes 512 | tf_op jit(solution)/shard_map/psum | solution.py:254
  (464 shorter events, 52.4 us)
Async XLA Ops:
  0.6 19.1 %copy-start.6 = (f32[3]{0:T(128)S(1)}, f32[3]{0:T(128)}, u32[]{:S(2)}) copy-start(f32[3]{0:T(128)} %constant.290.clone) | copy-start | bytes 40
  0.6 18.9 %copy-start.7 = (f32[4,3]{1,0:T(4,128)S(1)}, f32[4,3]{1,0:T(4,128)}, u32[]{:S(2)}) copy-start(f32[4,3]{1,0:T(4,128)} %constant.329) | copy-start | bytes 148
  0.7 19.3 %copy-start = (f32[1,2,256]{2,1,0:T(2,128)S(1)}, f32[1,2,256]{2,1,0:T(2,128)}, u32[]{:S(2)}) copy-start(f32[1,2,256]{2,1,0:T(2,128)} %param.22) | copy-start | bytes 6148
  0.7 19.3 %copy-start.1 = (s32[1,2,256]{2,1,0:T(2,128)S(1)}, s32[1,2,256]{2,1,0:T(2,128)}, u32[]{:S(2)}) copy-start(s32[1,2,256]{2,1,0:T(2,128)} %param.24) | copy-start | bytes 6148
  2.1 14.2 %collective-permute-start.4 = (f32[2,3,256]{2,1,0:T(4,128)S(1)}, f32[2,3,256]{2,1,0:T(4,128)S(1)}, u32[]{:S(2)}, u32[]{:S(2)}) collective-permute-start(f32[2,3,256]{2,1,0:T(4,128)S(1)} %bitcast_multiply_fusion.2), channel_id=1, source_target_pairs={{2,0},{4,2},{6,4},{8,6},{10,8},{12,10},{14,12},{0,14},{3,1},{5,3},... | collective-permute-start | bytes 18440 | tf_op jit(solution)/shard_map/ppermute | solution.py:19
  8.2 8.2 %collective-permute-start.5 = (f32[3,256]{1,0:T(4,128)S(1)}, f32[3,256]{1,0:T(4,128)S(1)}, u32[]{:S(2)}, u32[]{:S(2)}) collective-permute-start(f32[3,256]{1,0:T(4,128)S(1)} %get-tuple-element.1237), channel_id=1, source_target_pairs={{1,0},{0,1},{3,2},{2,3},{5,4},{4,5},{7,6},{6,7},{9,8},{8,9},{11,10... | collective-permute-start | bytes 9224 | tf_op jit(solution)/shard_map/ppermute | solution.py:19
  10.3 7.6 %collective-permute-start = (f32[2,5,256]{2,1,0:T(8,128)S(1)}, f32[2,5,256]{2,1,0:T(8,128)S(1)}, u32[]{:S(2)}, u32[]{:S(2)}) collective-permute-start(f32[2,5,256]{2,1,0:T(8,128)S(1)} %pad_maximum_fusion.4), channel_id=1, source_target_pairs={{2,0},{4,2},{6,4},{8,6},{10,8},{12,10},{14,12},{0,14},{3,1},{5,3},... | collective-permute-start | bytes 30728 | tf_op jit(solution)/shard_map/ppermute | solution.py:19
  10.9 6.1 %collective-permute-start.1 = (f32[5,256]{1,0:T(8,128)S(1)}, f32[5,256]{1,0:T(8,128)S(1)}, u32[]{:S(2)}, u32[]{:S(2)}) collective-permute-start(f32[5,256]{1,0:T(8,128)S(1)} %get-tuple-element.1225), channel_id=1, source_target_pairs={{1,0},{0,1},{3,2},{2,3},{5,4},{4,5},{7,6},{6,7},{9,8},{8,9},{11,10... | collective-permute-start | bytes 15368 | tf_op jit(solution)/shard_map/ppermute | solution.py:19
  16.4 1.2 collective-permute-start.7
  16.7 1.2 collective-permute-start.6
  17.9 1.2 collective-permute-start.3
  18.3 1.2 collective-permute-start.2
  19.9 23.8 %copy-start.3 = (f32[1,2,7,3,256]{4,1,3,2,0:T(2,128)S(1)}, f32[1,2,7,3,256]{4,1,3,2,0:T(2,128)}, u32[]{:S(2)}) copy-start(f32[1,2,7,3,256]{4,1,3,2,0:T(2,128)} %param.28) | copy-start | bytes 129028
  19.9 23.8 %copy-start.4 = (f32[1,2,7,3,256]{4,1,3,2,0:T(2,128)S(1)}, f32[1,2,7,3,256]{4,1,3,2,0:T(2,128)}, u32[]{:S(2)}) copy-start(f32[1,2,7,3,256]{4,1,3,2,0:T(2,128)} %param.27) | copy-start | bytes 129028
  19.9 31.1 %copy-start.2 = (f32[1,2,3,256]{3,1,2,0:T(2,128)S(1)}, f32[1,2,3,256]{3,1,2,0:T(2,128)}, u32[]{:S(2)}) copy-start(f32[1,2,3,256]{3,1,2,0:T(2,128)} %param.26) | copy-start | bytes 18436
  20.0 31.1 %copy-start.5 = (f32[1,2,3,256]{3,1,2,0:T(2,128)S(1)}, f32[1,2,3,256]{3,1,2,0:T(2,128)}, u32[]{:S(2)}) copy-start(f32[1,2,3,256]{3,1,2,0:T(2,128)} %param.25) | copy-start | bytes 18436
  43.1 1.2 collective-permute-start.10
  43.5 1.2 collective-permute-start.9
  43.7 2.5 collective-permute-start.8
  44.7 6.4 %collective-permute-start.11 = (f32[2,3,256]{2,1,0:T(4,128)S(1)}, f32[2,3,256]{2,1,0:T(4,128)S(1)}, u32[]{:S(2)}, u32[]{:S(2)}) collective-permute-start(f32[2,3,256]{2,1,0:T(4,128)S(1)} %fusion.77), channel_id=1, source_target_pairs={{14,0},{0,2},{2,4},{4,6},{6,8},{8,10},{10,12},{12,14},{15,1},{1,3}... | collective-permute-start | bytes 18440 | tf_op jit(solution)/shard_map/ppermute | solution.py:19
  130.4 3.9 %collective-permute-start.12 = (f32[2,3,256]{2,1,0:T(4,128)S(1)}, f32[2,3,256]{2,1,0:T(4,128)S(1)}, u32[]{:S(2)}, u32[]{:S(2)}) collective-permute-start(f32[2,3,256]{2,1,0:T(4,128)S(1)} %fusion.59), channel_id=1, source_target_pairs={{2,0},{4,2},{6,4},{8,6},{10,8},{12,10},{14,12},{0,14},{3,1},{5,3},... | collective-permute-start | bytes 18440 | tf_op jit(solution)/shard_map/ppermute | solution.py:19
  130.7 4.2 %collective-permute-start.13 = (f32[3,256]{1,0:T(4,128)S(1)}, f32[3,256]{1,0:T(4,128)S(1)}, u32[]{:S(2)}, u32[]{:S(2)}) collective-permute-start(f32[3,256]{1,0:T(4,128)S(1)} %get-tuple-element.1231), channel_id=1, source_target_pairs={{1,0},{0,1},{3,2},{2,3},{5,4},{4,5},{7,6},{6,7},{9,8},{8,9},{11,10... | collective-permute-start | bytes 9224 | tf_op jit(solution)/shard_map/ppermute | solution.py:19
  134.3 1.2 collective-permute-start.15
  134.3 1.3 collective-permute-start.14
  158.9 1.2 collective-permute-start.18
  159.3 1.2 collective-permute-start.17
  159.5 1.2 collective-permute-start.16
  160.5 6.4 %collective-permute-start.19 = (f32[2,3,256]{2,1,0:T(4,128)S(1)}, f32[2,3,256]{2,1,0:T(4,128)S(1)}, u32[]{:S(2)}, u32[]{:S(2)}) collective-permute-start(f32[2,3,256]{2,1,0:T(4,128)S(1)} %fusion.75), channel_id=1, source_target_pairs={{14,0},{0,2},{2,4},{4,6},{6,8},{8,10},{10,12},{12,14},{15,1},{1,3}... | collective-permute-start | bytes 18440 | tf_op jit(solution)/shard_map/ppermute | solution.py:19
  246.1 0.7 copy-start.8
where the time goes:
time: 249 us; the launch traced here: 247 us
  between operations  92.8 us (37%)
  blocking collectives  59 us (24%)
  other arithmetic  47 us (19%)
  waiting for transfers between devices  18.3 us (7%)
  local copies, waits for them, and re-layouts  15.3 us (6%)
  starting transfers between devices  12.4 us (5%)
    psum x2, blocking collectives, body(): gram_matrix = lax.psum(local_gram, ('gx', 'gy'))  59 us
    ppermute x20, waiting for transfers between devices, from_behind(): return lax.ppermute(block, axis, route)  18.3 us
    ppermute x20, starting transfers between devices, from_behind(): return lax.ppermute(block, axis, route)  12.4 us
    div x16, other arithmetic, pair_terms(): isotropic = weight * -jnp.expm1(-damped) / cube_dist  10.8 us
    reduce_sum x8, other arithmetic, field_sources(): projected = jnp.sum(displace * target_dipole[:, :, None], axis=0)  8.01 us
    mul x8, other arithmetic, field_targets(): tensorial * projected  7.77 us
    reduce_sum x8, other arithmetic, field_sources(): jnp.sum(displace * (tensorial * projected)[None], axis=1)  5.08 us
  transfers between devices with their start and end apart: 20, of which 14 were waited for; matrix products, arithmetic and copies ran while one was open for 3% of the time, Pallas kernels for 0%

commit v1 on v0

--- a/solution.py
+++ b/solution.py
@@ -251,7 +251,8 @@
             precision=lax.Precision.HIGHEST,
             preferred_element_type=jnp.float32,
         )
-        gram_matrix = lax.psum(local_gram, ("gx", "gy"))
+        launch_inputs = lambda mine: jax.lax.psum(jax.lax.psum(mine, "gy"), "gx")
+        gram_matrix = launch_inputs(local_gram)
         weights = diis_weights(gram_matrix)
         current = jnp.sum(weights[:, None, None, None] * outputs_all, axis=0)
         stored_out = outputs_all[1:]

time: 249 us -> 231 us (0.928)
  blocking collectives: 59 us -> 41.2 us
  waiting for transfers between devices: 18.3 us -> 13.5 us
  starting transfers between devices: 12.4 us -> 17.2 us
    psum x2 -> x4, blocking collectives: 59 us -> 41.2 us  [body(): launch_inputs = lambda mine: jax.lax.psum(jax.lax.psum(mine, 'gy'), 'gx')]
    ppermute x20, starting transfers between devices: 12.4 us -> 17.2 us  [from_behind(): return lax.ppermute(block, axis, route)]
    ppermute x20, waiting for transfers between devices: 18.3 us -> 13.5 us  [from_behind(): return lax.ppermute(block, axis, route)]
  transfers between devices with their start and end apart: 20 -> 20, of which waited for: 14 -> 13; matrix products, arithmetic and copies ran while one was open for 3% -> 3% of each run, Pallas kernels for 0% -> 0%
where the time goes in v1:
time: 231 us; the launch traced here: 229 us
  between operations  92.8 us (40%)
  other arithmetic  47 us (20%)
  blocking collectives  41.2 us (18%)
  starting transfers between devices  17.2 us (7%)
  local copies, waits for them, and re-layouts  15.3 us (7%)
  waiting for transfers between devices  13.5 us (6%)
    psum x4, blocking collectives, body(): launch_inputs = lambda mine: jax.lax.psum(jax.lax.psum(mine, 'gy'), 'gx')  41.2 us
    ppermute x20, starting transfers between devices, from_behind(): return lax.ppermute(block, axis, route)  17.2 us
    ppermute x20, waiting for transfers between devices, from_behind(): return lax.ppermute(block, axis, route)  13.5 us
    div x16, other arithmetic, pair_terms(): isotropic = weight * -jnp.expm1(-damped) / cube_dist  10.8 us
    reduce_sum x8, other arithmetic, field_sources(): projected = jnp.sum(displace * target_dipole[:, :, None], axis=0)  8.01 us
    mul x8, other arithmetic, field_targets(): tensorial * projected  7.77 us
    reduce_sum x8, other arithmetic, field_sources(): jnp.sum(displace * (tensorial * projected)[None], axis=1)  5.08 us
  transfers between devices with their start and end apart: 20, of which 13 were waited for; matrix products, arithmetic and copies ran while one was open for 3% of the time, Pallas kernels for 0%

profile of v1, /device:TPU:0, one launch (start us, length us, event | category | flops | bytes accessed | tf_op | source)
XLA Modules:
  0.0 229.0 jit_solution(10589178224206303825)
XLA Ops:
  2.1 6.0 %collective-permute-start.4 = (f32[2,3,256]{2,1,0:T(4,128)S(1)}, f32[2,3,256]{2,1,0:T(4,128)S(1)}, u32[]{:S(2)}, u32[]{:S(2)}) collective-permute-start(f32[2,3,256]{2,1,0:T(4,128)S(1)} %bitcast_multiply_fusion.2), channel_id=1, source_target_pairs={{2,0},{4,2},{6,4},{8,6},{10,8},{12,10},{14,12},{0,14},{3,1},{5,3},... | collective-permute-start | bytes 18440 | tf_op jit(solution)/shard_map/ppermute | solution.py:19
  20.0 23.1 %while.55 = (s32[]{:T(128)}, f32[2,3,256]{2,1,0:T(4,128)S(1)}, f32[2,4,3,256]{3,1,2,0:T(4,128)S(1)}, f32[2,3,256]{2,1,0:T(4,128)S(1)}, f32[2,256]{1,0:T(2,128)S(...) while((s32[]{:T(128)}, f32[2,3,256]{2,1,0:T(4,128)S(1)}, ...), condition=%wide.region_14.15_spmd, body=%wide.region_0.14_spmd.sunk | while | flops 19906180 | bytes 14344956 | solution.py:186
  20.2 11.3 %while.58 = (s32[]{:T(128)}, f32[3,256]{1,0:T(4,128)S(1)}, f32[4,3,4,128]{3,2,0,1:T(4,128)S(1)}, f32[1,3,4,128]{3,2,1,0:T(4,128)S(1)}, f32[3,256]{1,0:T(4,128)S(...) while((s32[]{:T(128)}, f32[3,256]{1,0:T(4,128)S(1)}, ...), condition=%wide.region_13.13_spmd, body=%wide.region_1.12_spmd.sunk | while | flops 19906180 | bytes 14031151 | solution.py:174
  21.9 1.0 fusion.153
  22.8 1.0 fusion.154
  27.5 1.0 fusion.153
  28.5 1.0 fusion.154
  31.7 11.3 %while.58 = (s32[]{:T(128)}, f32[3,256]{1,0:T(4,128)S(1)}, f32[4,3,4,128]{3,2,0,1:T(4,128)S(1)}, f32[1,3,4,128]{3,2,1,0:T(4,128)S(1)}, f32[3,256]{1,0:T(4,128)S(...) while((s32[]{:T(128)}, f32[3,256]{1,0:T(4,128)S(1)}, ...), condition=%wide.region_13.13_spmd, body=%wide.region_1.12_spmd.sunk | while | flops 19906180 | bytes 14031151 | solution.py:174
  33.4 1.0 fusion.153
  34.4 1.0 fusion.154
  39.0 1.0 fusion.153
  40.0 1.0 fusion.154
  44.7 1.5 collective-permute-start.11
  46.2 4.8 %collective-permute-done.11 = f32[2,3,256]{2,1,0:T(4,128)S(1)} collective-permute-done((f32[2,3,256]{2,1,0:T(4,128)S(1)}, f32[2,3,256]{2,1,0:T(4,128)S(1)}, u32[]{:S(2)}, u32[]{:S(2)}) %collective-permute-start.11) | collective-permute-done | bytes 6176 | tf_op jit(solution)/shard_map/ppermute | solution.py:19
  51.3 2.5 %psum.28 = f32[8,8]{0,1:T(8,128)S(1)} all-reduce(f32[8,8]{0,1:T(8,128)S(1)} %convolution_bitcast_fusion.1), channel_id=1, replica_groups=mesh['box'=2,'gx'=8,'gy'=2] {'gy'}, use_global_device_ids=true, to_apply=%region_15.16 | all-reduce | flops 64 | bytes 512 | tf_op jit(solution)/shard_map/psum | solution.py:254
  53.8 17.1 %psum.29 = f32[8,8]{0,1:T(8,128)S(1)} all-reduce(f32[8,8]{0,1:T(8,128)S(1)} %psum.28), channel_id=1, replica_groups=mesh['box'=2,'gx'=8,'gy'=2] {'gx'}, use_global_device_ids=true, to_apply=%region_16.17 | all-reduce | flops 64 | bytes 512 | tf_op jit(solution)/shard_map/psum | solution.py:254
  120.5 2.2 collective-permute-start.12
  122.7 1.6 collective-permute-done.12
  125.8 23.1 %while.57 = (s32[]{:T(128)}, f32[2,3,256]{2,1,0:T(4,128)S(1)}, f32[2,4,3,256]{3,1,2,0:T(4,128)S(1)}, f32[2,3,256]{2,1,0:T(4,128)S(1)}, f32[2,256]{1,0:T(2,128)S(...) while((s32[]{:T(128)}, f32[2,3,256]{2,1,0:T(4,128)S(1)}, ...), condition=%wide.region_34.36_spmd, body=%wide.region_20.35_spmd.sunk | while | flops 19906180 | bytes 14344960 | solution.py:186
  126.0 11.3 %while.59 = (s32[]{:T(128)}, f32[3,256]{1,0:T(4,128)S(1)}, f32[4,3,4,128]{3,2,0,1:T(4,128)S(1)}, f32[1,3,4,128]{3,2,1,0:T(4,128)S(1)}, f32[3,256]{1,0:T(4,128)S(...) while((s32[]{:T(128)}, f32[3,256]{1,0:T(4,128)S(1)}, ...), condition=%wide.region_33.34_spmd, body=%wide.region_21.33_spmd.sunk | while | flops 19906180 | bytes 14031151 | solution.py:174
  127.7 1.0 fusion.143
  128.7 1.0 fusion.144
  133.3 1.0 fusion.143
  134.3 1.0 fusion.144
  137.6 11.3 %while.59 = (s32[]{:T(128)}, f32[3,256]{1,0:T(4,128)S(1)}, f32[4,3,4,128]{3,2,0,1:T(4,128)S(1)}, f32[1,3,4,128]{3,2,1,0:T(4,128)S(1)}, f32[3,256]{1,0:T(4,128)S(...) while((s32[]{:T(128)}, f32[3,256]{1,0:T(4,128)S(1)}, ...), condition=%wide.region_33.34_spmd, body=%wide.region_21.33_spmd.sunk | while | flops 19906180 | bytes 14031151 | solution.py:174
  139.3 1.0 fusion.143
  140.2 1.0 fusion.144
  145.9 1.0 fusion.144
  150.6 3.0 %collective-permute-start.19 = (f32[2,3,256]{2,1,0:T(4,128)S(1)}, f32[2,3,256]{2,1,0:T(4,128)S(1)}, u32[]{:S(2)}, u32[]{:S(2)}) collective-permute-start(f32[2,3,256]{2,1,0:T(4,128)S(1)} %fusion.75), channel_id=1, source_target_pairs={{14,0},{0,2},{2,4},{4,6},{6,8},{8,10},{10,12},{12,14},{15,1},{1,3}... | collective-permute-start | bytes 18440 | tf_op jit(solution)/shard_map/ppermute | solution.py:19
  153.6 3.4 %collective-permute-done.19 = f32[2,3,256]{2,1,0:T(4,128)S(1)} collective-permute-done((f32[2,3,256]{2,1,0:T(4,128)S(1)}, f32[2,3,256]{2,1,0:T(4,128)S(1)}, u32[]{:S(2)}, u32[]{:S(2)}) %collective-permute-start.19) | collective-permute-done | bytes 6176 | tf_op jit(solution)/shard_map/ppermute | solution.py:19
  157.2 2.5 %psum.30 = f32[8,8]{0,1:T(8,128)S(1)} all-reduce(f32[8,8]{0,1:T(8,128)S(1)} %convolution_bitcast_fusion), channel_id=1, replica_groups=mesh['box'=2,'gx'=8,'gy'=2] {'gy'}, use_global_device_ids=true, to_apply=%region_35.37 | all-reduce | flops 64 | bytes 512 | tf_op jit(solution)/shard_map/psum | solution.py:254
  159.7 19.1 %psum.31 = f32[8,8]{0,1:T(8,128)S(1)} all-reduce(f32[8,8]{0,1:T(8,128)S(1)} %psum.30), channel_id=1, replica_groups=mesh['box'=2,'gx'=8,'gy'=2] {'gx'}, use_global_device_ids=true, to_apply=%region_36.38 | all-reduce | flops 64 | bytes 512 | tf_op jit(solution)/shard_map/psum | solution.py:254
  (466 shorter events, 55.8 us)
Async XLA Ops:
  0.6 19.1 %copy-start.6 = (f32[3]{0:T(128)S(1)}, f32[3]{0:T(128)}, u32[]{:S(2)}) copy-start(f32[3]{0:T(128)} %constant.290.clone) | copy-start | bytes 40
  0.6 18.9 %copy-start.7 = (f32[4,3]{1,0:T(4,128)S(1)}, f32[4,3]{1,0:T(4,128)}, u32[]{:S(2)}) copy-start(f32[4,3]{1,0:T(4,128)} %constant.329) | copy-start | bytes 148
  0.7 19.3 %copy-start = (f32[1,2,256]{2,1,0:T(2,128)S(1)}, f32[1,2,256]{2,1,0:T(2,128)}, u32[]{:S(2)}) copy-start(f32[1,2,256]{2,1,0:T(2,128)} %param.22) | copy-start | bytes 6148
  0.7 19.3 %copy-start.1 = (s32[1,2,256]{2,1,0:T(2,128)S(1)}, s32[1,2,256]{2,1,0:T(2,128)}, u32[]{:S(2)}) copy-start(s32[1,2,256]{2,1,0:T(2,128)} %param.24) | copy-start | bytes 6148
  2.1 14.2 %collective-permute-start.4 = (f32[2,3,256]{2,1,0:T(4,128)S(1)}, f32[2,3,256]{2,1,0:T(4,128)S(1)}, u32[]{:S(2)}, u32[]{:S(2)}) collective-permute-start(f32[2,3,256]{2,1,0:T(4,128)S(1)} %bitcast_multiply_fusion.2), channel_id=1, source_target_pairs={{2,0},{4,2},{6,4},{8,6},{10,8},{12,10},{14,12},{0,14},{3,1},{5,3},... | collective-permute-start | bytes 18440 | tf_op jit(solution)/shard_map/ppermute | solution.py:19
  8.2 8.2 %collective-permute-start.5 = (f32[3,256]{1,0:T(4,128)S(1)}, f32[3,256]{1,0:T(4,128)S(1)}, u32[]{:S(2)}, u32[]{:S(2)}) collective-permute-start(f32[3,256]{1,0:T(4,128)S(1)} %get-tuple-element.1237), channel_id=1, source_target_pairs={{1,0},{0,1},{3,2},{2,3},{5,4},{4,5},{7,6},{6,7},{9,8},{8,9},{11,10... | collective-permute-start | bytes 9224 | tf_op jit(solution)/shard_map/ppermute | solution.py:19
  10.3 7.6 %collective-permute-start = (f32[2,5,256]{2,1,0:T(8,128)S(1)}, f32[2,5,256]{2,1,0:T(8,128)S(1)}, u32[]{:S(2)}, u32[]{:S(2)}) collective-permute-start(f32[2,5,256]{2,1,0:T(8,128)S(1)} %pad_maximum_fusion.4), channel_id=1, source_target_pairs={{2,0},{4,2},{6,4},{8,6},{10,8},{12,10},{14,12},{0,14},{3,1},{5,3},... | collective-permute-start | bytes 30728 | tf_op jit(solution)/shard_map/ppermute | solution.py:19
  10.9 6.1 %collective-permute-start.1 = (f32[5,256]{1,0:T(8,128)S(1)}, f32[5,256]{1,0:T(8,128)S(1)}, u32[]{:S(2)}, u32[]{:S(2)}) collective-permute-start(f32[5,256]{1,0:T(8,128)S(1)} %get-tuple-element.1225), channel_id=1, source_target_pairs={{1,0},{0,1},{3,2},{2,3},{5,4},{4,5},{7,6},{6,7},{9,8},{8,9},{11,10... | collective-permute-start | bytes 15368 | tf_op jit(solution)/shard_map/ppermute | solution.py:19
  16.4 1.2 collective-permute-start.7
  16.7 1.2 collective-permute-start.6
  17.9 1.2 collective-permute-start.3
  18.3 1.2 collective-permute-start.2
  19.9 23.8 %copy-start.3 = (f32[1,2,7,3,256]{4,1,3,2,0:T(2,128)S(1)}, f32[1,2,7,3,256]{4,1,3,2,0:T(2,128)}, u32[]{:S(2)}) copy-start(f32[1,2,7,3,256]{4,1,3,2,0:T(2,128)} %param.28) | copy-start | bytes 129028
  19.9 23.8 %copy-start.4 = (f32[1,2,7,3,256]{4,1,3,2,0:T(2,128)S(1)}, f32[1,2,7,3,256]{4,1,3,2,0:T(2,128)}, u32[]{:S(2)}) copy-start(f32[1,2,7,3,256]{4,1,3,2,0:T(2,128)} %param.27) | copy-start | bytes 129028
  19.9 31.1 %copy-start.2 = (f32[1,2,3,256]{3,1,2,0:T(2,128)S(1)}, f32[1,2,3,256]{3,1,2,0:T(2,128)}, u32[]{:S(2)}) copy-start(f32[1,2,3,256]{3,1,2,0:T(2,128)} %param.26) | copy-start | bytes 18436
  20.0 31.1 %copy-start.5 = (f32[1,2,3,256]{3,1,2,0:T(2,128)S(1)}, f32[1,2,3,256]{3,1,2,0:T(2,128)}, u32[]{:S(2)}) copy-start(f32[1,2,3,256]{3,1,2,0:T(2,128)} %param.25) | copy-start | bytes 18436
  43.1 1.2 collective-permute-start.10
  43.5 1.2 collective-permute-start.9
  43.7 2.5 %collective-permute-start.8 = (f32[3,256]{1,0:T(4,128)S(1)}, f32[3,256]{1,0:T(4,128)S(1)}, u32[]{:S(2)}, u32[]{:S(2)}) collective-permute-start(f32[3,256]{1,0:T(4,128)S(1)} %get-tuple-element.1218), channel_id=1, source_target_pairs={{1,0},{0,1},{3,2},{2,3},{5,4},{4,5},{7,6},{6,7},{9,8},{8,9},{11,10... | collective-permute-start | bytes 9224 | tf_op jit(solution)/shard_map/ppermute | solution.py:19
  44.7 6.4 %collective-permute-start.11 = (f32[2,3,256]{2,1,0:T(4,128)S(1)}, f32[2,3,256]{2,1,0:T(4,128)S(1)}, u32[]{:S(2)}, u32[]{:S(2)}) collective-permute-start(f32[2,3,256]{2,1,0:T(4,128)S(1)} %fusion.77), channel_id=1, source_target_pairs={{14,0},{0,2},{2,4},{4,6},{6,8},{8,10},{10,12},{12,14},{15,1},{1,3}... | collective-permute-start | bytes 18440 | tf_op jit(solution)/shard_map/ppermute | solution.py:19
  120.5 3.9 %collective-permute-start.12 = (f32[2,3,256]{2,1,0:T(4,128)S(1)}, f32[2,3,256]{2,1,0:T(4,128)S(1)}, u32[]{:S(2)}, u32[]{:S(2)}) collective-permute-start(f32[2,3,256]{2,1,0:T(4,128)S(1)} %fusion.59), channel_id=1, source_target_pairs={{2,0},{4,2},{6,4},{8,6},{10,8},{12,10},{14,12},{0,14},{3,1},{5,3},... | collective-permute-start | bytes 18440 | tf_op jit(solution)/shard_map/ppermute | solution.py:19
  122.7 2.2 collective-permute-start.13
  124.4 1.2 collective-permute-start.15
  124.4 1.3 collective-permute-start.14
  149.0 1.2 collective-permute-start.18
  149.4 1.2 collective-permute-start.17
  149.6 4.0 %collective-permute-start.16 = (f32[3,256]{1,0:T(4,128)S(1)}, f32[3,256]{1,0:T(4,128)S(1)}, u32[]{:S(2)}, u32[]{:S(2)}) collective-permute-start(f32[3,256]{1,0:T(4,128)S(1)} %get-tuple-element.1213), channel_id=1, source_target_pairs={{1,0},{0,1},{3,2},{2,3},{5,4},{4,5},{7,6},{6,7},{9,8},{8,9},{11,10... | collective-permute-start | bytes 9224 | tf_op jit(solution)/shard_map/ppermute | solution.py:19
  150.6 6.4 %collective-permute-start.19 = (f32[2,3,256]{2,1,0:T(4,128)S(1)}, f32[2,3,256]{2,1,0:T(4,128)S(1)}, u32[]{:S(2)}, u32[]{:S(2)}) collective-permute-start(f32[2,3,256]{2,1,0:T(4,128)S(1)} %fusion.75), channel_id=1, source_target_pairs={{14,0},{0,2},{2,4},{4,6},{6,8},{8,10},{10,12},{12,14},{15,1},{1,3}... | collective-permute-start | bytes 18440 | tf_op jit(solution)/shard_map/ppermute | solution.py:19
  228.3 0.7 copy-start.8
